TPU v7x, 256 devices: a whole 4x4x8 slice. The times are simulated.
256 devices in a mesh: leaf: 128 (over x, y, z), col: 2 (over core).
Axes of the slice: x: 4, y: 4, z: 8, core: 2. Of those that a mesh axis runs over, the one named last changes fastest.
Arguments:
- coords: float32 [3, 262144], P(None, 'leaf'), may hold values from -6 to 6
- values: float32 [32, 262144], P('col', 'leaf'), may hold values from -6 to 6
- leaf_basis: float32 [1024, 256, 128], P('leaf'), may hold values from -0.375 to 0.375
- leaf_transfer: float32 [1024, 128, 128], P('leaf'), may hold values from -0.1875 to 0.1875
- node_transfer: float32 [128, 128, 128], P('leaf'), may hold values from -0.1875 to 0.1875
- leaf_coupling: float32 [1024, 8, 128, 128], P('leaf', None, 'col'), may hold values from -0.1875 to 0.1875
- node_coupling: float32 [128, 2, 128, 128], P('leaf', None, 'col'), may hold values from -0.375 to 0.375
- top_coupling: float32 [16, 4, 128, 128], P(None, None, 'col'), may hold values from -0.25 to 0.25
- near_list: int32 [1024, 8], P('leaf'), may hold values from -1 to 1023, as said below
- leaf_list: int32 [1024, 8], P('leaf'), may hold values from -1 to 1023, as said below
- node_list: int32 [128, 2], P('leaf'), may hold values from -1 to 127, as said below
- top_list: int32 [16, 4], replicated, may hold values from -1 to 15, as said below
Outputs:
- adjoint_product: float32 [32, 262144], P('col', 'leaf')
Inputs may be any that keep to these rules, and one draw needn't show every extreme that they name: `leaf_list`: leaf l names only leaves other than itself on devices l // 8 - 1 to l // 8 + 1 of a Morton order of 8 leaves a device; slot 0 is live, live slots come first, and some leaf fills all 8 slots. `near_list`: leaf l names only leaves (itself allowed) on devices l // 8 - 1 to l // 8 + 1; slot 0 is live, live slots come first, and some leaf fills all 8 slots. `node_list`: node p names only nodes p - 1 and p + 1; slot 0 is live, live slots come first, and some node fills all 2 slots. `top_list`: top node g may name any top node, itself allowed; slot 0 is live, live slots come first, and some top node fills all 4 slots.
All inputs are finite; a program needn't handle non-finite values.
Results may differ from a plain program's by a relative error of at most 0.0003.
Values sent between devices are 32-bit elements; how exact they have to be, the bound alone decides.
A program may use at most 64 MiB of HBM per device.

v0:
```python
import math
import jax
import jax.numpy as jnp
from jax import lax
from jax.sharding import PartitionSpec as P

SOFTENING = 0.01


def extended_2(x, sides, width):
    for axis, dim in sides:
        devices, length = (lax.axis_size(axis), x.shape[dim])
        up = [(i, (i + 1) % devices) for i in range(devices - 1)]
        down = [(j, i) for i, j in up]
        last = lax.slice_in_dim(x, length - width, length, axis=dim)
        leading = lax.slice_in_dim(x, 0, width, axis=dim)
        before = lax.ppermute(last, axis, up)
        after = lax.ppermute(leading, axis, down)
        x = jnp.concatenate([before, x, after], axis=dim)
    return x


def couple(blocks, local_index, sources):
    high = lax.Precision.HIGHEST
    live_mask = (local_index >= 0).astype(jnp.float32)
    safe_index = jnp.maximum(local_index, 0)
    wide_moments = lax.all_gather(sources, "col", axis=1, tiled=True)
    half_rank = blocks.shape[2]
    rank_start = lax.axis_index("col") * half_rank
    rank_part = lax.dynamic_slice_in_dim(wide_moments, rank_start, half_rank, 2)
    picked = jnp.take(rank_part, safe_index, axis=0) * live_mask[:, :, None, None]
    partial_value = jnp.einsum("nsca,nsab->ncb", picked, blocks, precision=high)
    return lax.psum_scatter(partial_value, "col", scatter_dimension=1, tiled=True)


def body(
    coords,
    values,
    leaf_basis,
    leaf_transfer,
    node_transfer,
    leaf_coupling,
    node_coupling,
    top_coupling,
    near_list,
    leaf_list,
    node_list,
    top_list,
):
    high = lax.Precision.HIGHEST
    device = lax.axis_index("leaf")
    per_device = leaf_basis.shape[0]
    points = leaf_basis.shape[1]
    core_cols = values.shape[0]
    rank_width = leaf_basis.shape[2]
    leaf_values = values.reshape(core_cols, per_device, points)
    leaf_moments = jnp.einsum("lpr,clp->lcr", leaf_basis, leaf_values, precision=high)
    node_moments = jnp.einsum("lab,lca->cb", leaf_transfer, leaf_moments, precision=high)[None]
    contrib = jnp.einsum("nab,nca->ncb", node_transfer, node_moments, precision=high)
    top_count = lax.axis_size("leaf") // 8
    everything = lax.all_gather(contrib, "leaf", axis=0, tiled=True)
    top_moments = everything.reshape(top_count, 8, core_cols, rank_width).sum(axis=1)
    top_node = device // 8
    top_rows = lax.dynamic_slice_in_dim(top_coupling, top_node, 1, 0)
    top_index = lax.dynamic_slice_in_dim(top_list, top_node, 1, 0)
    top_local = couple(top_rows, top_index, top_moments)
    node_ext = extended_2(node_moments, (("leaf", 0),), 1)
    node_index = jnp.where(node_list >= 0, node_list - (device - 1), -1)
    node_local = couple(node_coupling, node_index, node_ext) + jnp.einsum(
        "nab,ncb->nca", node_transfer, top_local, precision=high
    )
    leaf_ext = extended_2(leaf_moments, (("leaf", 0),), per_device)
    leaf_index = jnp.where(leaf_list >= 0, leaf_list - (device - 1) * per_device, -1)
    leaf_local = couple(leaf_coupling, leaf_index, leaf_ext) + jnp.einsum(
        "lab,cb->lca", leaf_transfer, node_local[0], precision=high
    )
    far_field = jnp.einsum("lpr,lcr->clp", leaf_basis, leaf_local, precision=high)
    leaf_rows = jnp.concatenate((coords, values), axis=0)
    extended = extended_2(leaf_rows, (("leaf", 1),), per_device * points)
    extended = extended.reshape(3 + core_cols, 3 * per_device, points)
    near_index = jnp.where(near_list >= 0, near_list - (device - 1) * per_device, -1)
    target = coords.reshape(3, per_device, points)
    scale = 1.0 / math.sqrt(points)
    near_field = jnp.zeros((per_device, core_cols, points), jnp.float32)
    for slot_index in range(near_list.shape[1]):
        column = near_index[:, slot_index]
        live_mask = (column >= 0).astype(jnp.float32)
        source_rows = jnp.take(extended, jnp.maximum(column, 0), axis=1)
        offset_sq = jnp.sum((target[:, :, :, None] - source_rows[:3, :, None, :]) ** 2, axis=0)
        kernel = scale / jnp.sqrt(offset_sq + SOFTENING)
        term = jnp.einsum("lab,clb->lca", kernel, source_rows[3:], precision=high)
        near_field = near_field + live_mask[:, None, None] * term
    total = jnp.transpose(near_field, (1, 0, 2)) + far_field
    return total.reshape(core_cols, per_device * points)


def solution(mesh):
    in_specs = (
        P(None, "leaf"),
        P("col", "leaf"),
        P("leaf", None, None),
        P("leaf", None, None),
        P("leaf", None, None),
        P("leaf", None, "col", None),
        P("leaf", None, "col", None),
        P(None, None, "col", None),
        P("leaf", None),
        P("leaf", None),
        P("leaf", None),
        P(),
    )
    out_specs = P("col", "leaf")
    return jax.shard_map(body, mesh=mesh, in_specs=in_specs, out_specs=out_specs, check_vma=False)
```

profile of v0, /device:TPU:1, one launch (start us, length us, event | category | flops | bytes accessed | tf_op | source)
XLA Modules:
  0.0 207.8 jit_solution(12631651173582469412)
XLA Ops:
  7.5 1.8 pad_maximum_fusion.1
  9.2 5.0 %collective-permute-start = (f32[19,2048]{1,0:T(8,128)}, f32[19,2048]{1,0:T(8,128)}, u32[]{:S(2)}, u32[]{:S(2)}) collective-permute-start(f32[19,2048]{1,0:T(8,128)} %pad_maximum_fusion.1), channel_id=1, source_target_pairs={{0,2},{2,4},{4,6},{6,8},{8,10},{10,12},{12,14},{14,16},{16,18},{18... | collective-permute-start | bytes 466952 | tf_op jit(solution)/shard_map/ppermute | solution.py:17
  14.3 1.3 collective-permute-start.1
  15.5 1.9 fusion.107
  17.5 1.4 fusion.159
  18.9 4.0 %collective-permute-start.4 = (f32[1,16,128]{2,1,0:T(8,128)S(1)}, f32[1,16,128]{2,1,0:T(8,128)S(1)}, u32[]{:S(2)}, u32[]{:S(2)}) collective-permute-start(f32[1,16,128]{2,1,0:T(8,128)S(1)} %bitcast.94), channel_id=1, source_target_pairs={{0,2},{2,4},{4,6},{6,8},{8,10},{10,12},{12,14},{14,16},{16,18},{18... | collective-permute-start | bytes 24584 | tf_op jit(solution)/shard_map/ppermute | solution.py:17
  22.9 1.3 collective-permute-start.5
  24.2 4.0 %collective-permute-start.2 = (f32[8,16,128]{2,1,0:T(8,128)S(1)}, f32[8,16,128]{2,1,0:T(8,128)S(1)}, u32[]{:S(2)}, u32[]{:S(2)}) collective-permute-start(f32[8,16,128]{2,1,0:T(8,128)S(1)} %fusion.107), channel_id=1, source_target_pairs={{0,2},{2,4},{4,6},{6,8},{8,10},{10,12},{12,14},{14,16},{16,18},{18... | collective-permute-start | bytes 196616 | tf_op jit(solution)/shard_map/ppermute | solution.py:17
  28.2 0.8 fusion.121
  34.5 0.8 convert_reduce_fusion
  38.8 0.7 convert_reduce_fusion.8
  39.5 0.8 compare_reduce_fusion
  40.3 1.3 collective-permute-start.3
  41.6 3.6 %all_gather.13 = f32[3,32,128]{2,1,0:T(8,128)S(1)} all-gather(f32[3,16,128]{2,1,0:T(8,128)S(1)} %pad_maximum_fusion.3), channel_id=1, replica_groups=mesh['leaf'=128,'col'=2] {'col'}, dimensions={1}, use_global_device_ids=true | all-gather | bytes 73728 | tf_op jit(solution)/shard_map/all_gather | solution.py:27
  45.8 0.9 convolution_bitcast_fusion.3
  46.8 3.7 %all_gather.12 = f32[24,32,128]{2,1,0:T(8,128)S(1)} all-gather(f32[24,16,128]{2,1,0:T(8,128)S(1)} %pad_maximum_fusion.2), channel_id=1, replica_groups=mesh['leaf'=128,'col'=2] {'col'}, dimensions={1}, use_global_device_ids=true | all-gather | bytes 589824 | tf_op jit(solution)/shard_map/all_gather | solution.py:27
  51.3 84.4 %all-gather.3.cloned.1.call-done = f32[2048,128]{1,0:T(8,128)} async-done(((f32[16,128]{1,0:T(8,128)}), f32[2048,128]{1,0:T(8,128)}) %all-gather.3.cloned.1.call-update) | async-done | bytes 1048592 | tf_op jit(solution)/shard_map/all_gather | solution.py:61
  135.7 1.3 reduce_sum.89
  137.0 7.1 %all_gather.15 = f32[16,32,128]{2,1,0:T(8,128)S(1)} all-gather(f32[16,16,128]{2,1,0:T(8,128)S(1)} %reduce_sum.89), channel_id=1, replica_groups=mesh['leaf'=128,'col'=2] {'col'}, dimensions={1}, use_global_device_ids=true | all-gather | bytes 393216 | tf_op jit(solution)/shard_map/all_gather | solution.py:27
  144.3 1.3 gather_fusion.2
  145.6 1.9 convolution_bitcast_fusion.2
  147.5 2.1 %convolution_bitcast_fusion = f32[8,32,128]{2,1,0:T(8,128)} fusion(f32[8,8,64,128]{3,2,1,0:T(8,128)S(1)} %copy-done, f32[8,8,32,64]{3,2,1,0:T(8,128)S(1)} %bitcast.87, f32[8,8]{1,0:T(8,128)S(1)} %get-tuple-element.34, pred[8,8]{1,0:T(8,128)(4,1)S(1)} %copy-done.17), kind=kOutput, calls=%fused_computation.68 | convolution fusion | flops 201588736 | bytes 2752832 | tf_op jit(solution)/shard_map/nsca,nsab->ncb/dot_general | solution.py:32
  149.8 1.1 pad_maximum_fusion
  151.3 0.7 gather_fusion.4
  152.7 0.7 gather_fusion.5
  154.1 0.7 gather_fusion.6
  154.9 0.7 copy-done.3
  156.2 0.7 gather_fusion.7
  156.9 0.7 select_bitcast_fusion.3
  158.2 0.7 gather_fusion.8
  160.3 0.7 gather_fusion.9
  162.9 0.8 select_bitcast_fusion.7
  163.7 0.7 copy-done.9
  164.9 1.2 gather_fusion.10
  166.2 1.0 select_bitcast_fusion
  167.2 11.0 %multiply_reduce_fusion = (f32[8,256,256]{2,1,0:T(8,128)}, f32[8,256,256]{2,1,0:T(8,128)S(1)}, f32[8,256,256]{2,1,0:T(8,128)S(1)}, f32[8,256,256]{2,1,0:T(8,128)...) fusion(f32[3,8,256]{2,1,0:T(8,128)S(1)} %copy.65, ...), kind=kLoop, calls=%fused_computation.11 | loop fusion | flops 33554432 | bytes 16998400 | tf_op jit(solution)/shard_map/reduce_sum | solution.py:89
  178.3 1.9 fusion.44
  180.2 1.9 fusion.47
  182.1 1.9 fusion.50
  184.1 1.9 fusion.65
  186.0 1.9 fusion.68
  187.9 1.9 fusion.41
  189.9 2.6 %fusion.62 = f32[8,16,256]{2,1,0:T(8,128)} fusion(f32[8,16,256]{2,1,0:T(8,128)S(1)} %fusion.68, f32[8,16,256]{2,1,0:T(8,128)S(1)} %fusion.65, f32[8,16,256]{2,1,0:T(8,128)S(1)} %fusion.41, f32[8,256,256]{2,1,0:T(8,128)S(1)} %get-tuple-element.10, f32[19,8,256]{2,0,1:T(8,128)S(1)} %select_bitcast_fusion.3, f32[8]{0:T(128)S(1)} %copy-done.20), kind=kOutput, calls=%fused_computation.61 | convolution fusion | flops 101842944 | bytes 2753024 | tf_op jit(solution)/shard_map/lab,clb->lca/dot_general | solution.py:91
  192.4 1.0 fusion.85
  193.5 1.6 fusion.83
  195.1 1.0 fusion.160
  196.1 3.5 %fusion.80 = f32[8,2,8,256]{3,2,1,0:T(8,128)S(1)} fusion(f32[8,16,256]{2,1,0:T(8,128)S(1)} %fusion.160, f32[8,16,256]{2,1,0:T(8,128)} %fusion.62, f32[8,256,256]{2,1,0:T(8,128)} %get-tuple-element.6, f32[19,8,256]{2,0,1:T(8,128)S(1)} %select_bitcast_fusion, f32[8]{0:T(128)S(1)} %copy-done.32), kind=kOutput, calls=%fused_computation.67 | convolution fusion | flops 101810176 | bytes 2621952 | tf_op jit(solution)/shard_map/lab,clb->lca/dot_general | solution.py:91
  199.6 0.7 copy.70
  (144 shorter events, 17.9 us)
Async XLA Ops:
  7.4 140.1 %copy-start = (f32[8,8,64,128]{3,2,1,0:T(8,128)S(1)}, f32[8,8,64,128]{3,2,1,0:T(8,128)}, u32[]{:S(2)}) copy-start(f32[8,8,64,128]{3,2,1,0:T(8,128)} %param.19) | copy-start | bytes 6291460
  7.4 30.8 %copy-start.11 = (f32[3,2048]{1,0:T(4,128)S(1)}, f32[3,2048]{1,0:T(4,128)}, u32[]{:S(2)}) copy-start(f32[3,2048]{1,0:T(4,128)} %param.14) | copy-start | bytes 73732
  7.4 20.8 %copy-start.13 = (f32[1,128,128]{2,1,0:T(8,128)S(1)}, f32[1,128,128]{2,1,0:T(8,128)}, u32[]{:S(2)}) copy-start(f32[1,128,128]{2,1,0:T(8,128)} %param.18) | copy-start | bytes 196612
  7.4 21.7 %copy-start.19 = (s32[8,8]{1,0:T(8,128)S(1)}, s32[8,8]{1,0:T(8,128)}, u32[]{:S(2)}) copy-start(s32[8,8]{1,0:T(8,128)} %param.22) | copy-start | bytes 772
  7.4 25.6 %copy-start.16 = (s32[16,4]{0,1:T(4,128)S(1)}, s32[16,4]{0,1:T(4,128)}, u32[]{:S(2)}) copy-start(s32[16,4]{0,1:T(4,128)} %param.25) | copy-start | bytes 772
  7.4 26.4 %copy-start.33 = (s32[1,2]{1,0:T(1,128)S(1)}, s32[1,2]{1,0:T(1,128)}, u32[]{:S(2)}) copy-start(s32[1,2]{1,0:T(1,128)} %param.24) | copy-start | bytes 28
  7.4 26.4 %copy-start.18 = (s32[8,8]{1,0:T(8,128)S(1)}, s32[8,8]{1,0:T(8,128)}, u32[]{:S(2)}) copy-start(s32[8,8]{1,0:T(8,128)} %param.23) | copy-start | bytes 772
  7.4 38.4 %copy-start.15 = (f32[1,2,64,128]{3,2,1,0:T(8,128)S(1)}, f32[1,2,64,128]{3,2,1,0:T(8,128)}, u32[]{:S(2)}) copy-start(f32[1,2,64,128]{3,2,1,0:T(8,128)} %param.20) | copy-start | bytes 196612
  7.4 128.3 %all-gather.3.cloned.1.call-start = ((), (), s32[]{:S(2)}) async-start(), calls=%async_computation.6 | async-start | bytes 1056768 | tf_op jit(solution)/shard_map/all_gather | solution.py:61
  9.2 140.5 %collective-permute-start = (f32[19,2048]{1,0:T(8,128)}, f32[19,2048]{1,0:T(8,128)}, u32[]{:S(2)}, u32[]{:S(2)}) collective-permute-start(f32[19,2048]{1,0:T(8,128)} %pad_maximum_fusion.1), channel_id=1, source_target_pairs={{0,2},{2,4},{4,6},{6,8},{8,10},{10,12},{12,14},{14,16},{16,18},{18... | collective-permute-start | bytes 466952 | tf_op jit(solution)/shard_map/ppermute | solution.py:17
  14.3 135.5 %collective-permute-start.1 = (f32[19,2048]{1,0:T(8,128)}, f32[19,2048]{1,0:T(8,128)}, u32[]{:S(2)}, u32[]{:S(2)}) collective-permute-start(f32[19,2048]{1,0:T(8,128)} %pad_maximum_fusion.1), channel_id=1, source_target_pairs={{2,0},{4,2},{6,4},{8,6},{10,8},{12,10},{14,12},{16,14},{18,16},{20... | collective-permute-start | bytes 466952 | tf_op jit(solution)/shard_map/ppermute | solution.py:18
  18.9 21.4 %collective-permute-start.4 = (f32[1,16,128]{2,1,0:T(8,128)S(1)}, f32[1,16,128]{2,1,0:T(8,128)S(1)}, u32[]{:S(2)}, u32[]{:S(2)}) collective-permute-start(f32[1,16,128]{2,1,0:T(8,128)S(1)} %bitcast.94), channel_id=1, source_target_pairs={{0,2},{2,4},{4,6},{6,8},{8,10},{10,12},{12,14},{14,16},{16,18},{18... | collective-permute-start | bytes 24584 | tf_op jit(solution)/shard_map/ppermute | solution.py:17
  22.9 18.7 %collective-permute-start.5 = (f32[1,16,128]{2,1,0:T(8,128)S(1)}, f32[1,16,128]{2,1,0:T(8,128)S(1)}, u32[]{:S(2)}, u32[]{:S(2)}) collective-permute-start(f32[1,16,128]{2,1,0:T(8,128)S(1)} %bitcast.95), channel_id=1, source_target_pairs={{2,0},{4,2},{6,4},{8,6},{10,8},{12,10},{14,12},{16,14},{18,16},{20... | collective-permute-start | bytes 24584 | tf_op jit(solution)/shard_map/ppermute | solution.py:18
  24.2 22.6 %collective-permute-start.2 = (f32[8,16,128]{2,1,0:T(8,128)S(1)}, f32[8,16,128]{2,1,0:T(8,128)S(1)}, u32[]{:S(2)}, u32[]{:S(2)}) collective-permute-start(f32[8,16,128]{2,1,0:T(8,128)S(1)} %fusion.107), channel_id=1, source_target_pairs={{0,2},{2,4},{4,6},{6,8},{8,10},{10,12},{12,14},{14,16},{16,18},{18... | collective-permute-start | bytes 196616 | tf_op jit(solution)/shard_map/ppermute | solution.py:17
  29.0 163.4 %reduce-scatter.6.cloned.1.call-start = ((), (), s32[]{:S(2)}) async-start(), calls=%async_computation.4 | async-start | bytes 24576 | tf_op jit(solution)/shard_map/reduce_scatter | solution.py:33
  40.3 6.5 %collective-permute-start.3 = (f32[8,16,128]{2,1,0:T(8,128)S(1)}, f32[8,16,128]{2,1,0:T(8,128)S(1)}, u32[]{:S(2)}, u32[]{:S(2)}) collective-permute-start(f32[8,16,128]{2,1,0:T(8,128)S(1)} %fusion.107), channel_id=1, source_target_pairs={{2,0},{4,2},{6,4},{8,6},{10,8},{12,10},{14,12},{16,14},{18,16},{20... | collective-permute-start | bytes 196616 | tf_op jit(solution)/shard_map/ppermute | solution.py:18
  46.7 145.7 %reduce-scatter.8.cloned.1.call-start = ((), (), s32[]{:S(2)}) async-start(), calls=%async_computation.5 | async-start | bytes 24576 | tf_op jit(solution)/shard_map/reduce_scatter | solution.py:33
  51.3 96.2 %copy-start.17 = (pred[8,8]{1,0:T(8,128)(4,1)S(1)}, pred[8,8]{1,0:T(8,128)(4,1)}, u32[]{:S(2)}) copy-start(pred[8,8]{1,0:T(8,128)(4,1)} %get-tuple-element.32) | copy-start | bytes 196
  144.1 5.6 %copy-start.2 = (f32[16,2048]{1,0:T(8,128)S(1)}, f32[16,2048]{1,0:T(8,128)}, u32[]{:S(2)}) copy-start(f32[16,2048]{1,0:T(8,128)} %param.15) | copy-start | bytes 393220
  145.6 4.2 %copy-start.12 = (f32[3,2048]{1,0:T(4,128)S(1)}, f32[3,2048]{1,0:T(4,128)}, u32[]{:S(2)}) copy-start(f32[3,2048]{1,0:T(4,128)} %param.14) | copy-start | bytes 73732
  147.5 46.0 %reduce-scatter.4.cloned.1.call-start = ((), (), s32[]{:S(2)}) async-start(), calls=%async_computation.3 | async-start | bytes 196608 | tf_op jit(solution)/shard_map/reduce_scatter | solution.py:33
  149.7 2.3 %copy-start.31 = (pred[8]{0:T(512)(128)(4,1)S(1)}, pred[8]{0:T(512)(128)(4,1)}, u32[]{:S(2)}) copy-start(pred[8]{0:T(512)(128)(4,1)} %get-tuple-element.48) | copy-start | bytes 28
  150.8 2.5 %copy-start.30 = (pred[8]{0:T(512)(128)(4,1)S(1)}, pred[8]{0:T(512)(128)(4,1)}, u32[]{:S(2)}) copy-start(pred[8]{0:T(512)(128)(4,1)} %get-tuple-element.47) | copy-start | bytes 28
  151.0 3.7 %copy-start.29 = (pred[8]{0:T(512)(128)(4,1)S(1)}, pred[8]{0:T(512)(128)(4,1)}, u32[]{:S(2)}) copy-start(pred[8]{0:T(512)(128)(4,1)} %get-tuple-element.46) | copy-start | bytes 28
  151.1 7.8 %copy-start.28 = (pred[8]{0:T(512)(128)(4,1)S(1)}, pred[8]{0:T(512)(128)(4,1)}, u32[]{:S(2)}) copy-start(pred[8]{0:T(512)(128)(4,1)} %get-tuple-element.44) | copy-start | bytes 28
  152.0 9.0 %copy-start.27 = (pred[8]{0:T(512)(128)(4,1)S(1)}, pred[8]{0:T(512)(128)(4,1)}, u32[]{:S(2)}) copy-start(pred[8]{0:T(512)(128)(4,1)} %get-tuple-element.43) | copy-start | bytes 28
  154.9 0.7 copy-start.3
  155.6 11.6 %copy-start.14 = (f32[1,3,8,256]{3,2,1,0:T(8,128)S(1)}, f32[1,3,8,256]{3,2,1,0:T(8,128)}, u32[]{:S(2)}) copy-start(f32[1,3,8,256]{3,2,1,0:T(8,128)} %copy.78) | copy-start | bytes 73732
  159.0 0.7 copy-start.5
  161.0 0.7 copy-start.7
  163.7 0.7 copy-start.9
  167.2 11.0 %copy-start.26 = (f32[8]{0:T(128)S(1)}, f32[8]{0:T(128)}, u32[]{:S(2)}) copy-start(f32[8]{0:T(128)} %get-tuple-element.20) | copy-start | bytes 100
  178.3 1.9 copy-start.25
  178.3 3.8 %copy-start.4 = (f32[19,8,256]{2,0,1:T(8,128)S(1)}, f32[19,8,256]{2,0,1:T(8,128)}, u32[]{:S(2)}) copy-start(f32[19,8,256]{2,0,1:T(8,128)} %copy-done.3) | copy-start | bytes 466948
  178.3 3.8 %copy-start.24 = (f32[8]{0:T(128)S(1)}, f32[8]{0:T(128)}, u32[]{:S(2)}) copy-start(f32[8]{0:T(128)} %get-tuple-element.18) | copy-start | bytes 100
  180.2 3.9 %copy-start.6 = (f32[19,8,256]{2,0,1:T(8,128)S(1)}, f32[19,8,256]{2,0,1:T(8,128)}, u32[]{:S(2)}) copy-start(f32[19,8,256]{2,0,1:T(8,128)} %copy-done.5) | copy-start | bytes 466948
  180.2 3.9 %copy-start.23 = (f32[8]{0:T(128)S(1)}, f32[8]{0:T(128)}, u32[]{:S(2)}) copy-start(f32[8]{0:T(128)} %get-tuple-element.16) | copy-start | bytes 100
  182.1 3.9 %copy-start.8 = (f32[19,8,256]{2,0,1:T(8,128)S(1)}, f32[19,8,256]{2,0,1:T(8,128)}, u32[]{:S(2)}) copy-start(f32[19,8,256]{2,0,1:T(8,128)} %copy-done.7) | copy-start | bytes 466948
  182.1 3.9 %copy-start.22 = (f32[8]{0:T(128)S(1)}, f32[8]{0:T(128)}, u32[]{:S(2)}) copy-start(f32[8]{0:T(128)} %get-tuple-element.15) | copy-start | bytes 100
  184.0 3.8 %copy-start.10 = (f32[19,8,256]{2,0,1:T(8,128)S(1)}, f32[19,8,256]{2,0,1:T(8,128)}, u32[]{:S(2)}) copy-start(f32[19,8,256]{2,0,1:T(8,128)} %copy-done.9) | copy-start | bytes 466948
  184.1 3.8 %copy-start.21 = (f32[8]{0:T(128)S(1)}, f32[8]{0:T(128)}, u32[]{:S(2)}) copy-start(f32[8]{0:T(128)} %get-tuple-element.21) | copy-start | bytes 100
  186.0 3.9 %copy-start.20 = (f32[8]{0:T(128)S(1)}, f32[8]{0:T(128)}, u32[]{:S(2)}) copy-start(f32[8]{0:T(128)} %get-tuple-element.17) | copy-start | bytes 100
  189.8 5.3 %copy-start.1 = (f32[8,256,128]{2,1,0:T(8,128)S(1)}, f32[8,256,128]{2,1,0:T(8,128)}, u32[]{:S(2)}) copy-start(f32[8,256,128]{2,1,0:T(8,128)} %param.16) | copy-start | bytes 3145732
  189.8 6.2 %copy-start.32 = (f32[8]{0:T(128)S(1)}, f32[8]{0:T(128)}, u32[]{:S(2)}) copy-start(f32[8]{0:T(128)} %get-tuple-element.14) | copy-start | bytes 100
Sparse Core Ops, SparseCore 0:
  29.1 106.5 all-gather.2
Sparse Core Ops, SparseCore 1:
  46.8 21.7 reduce-scatter.5
  147.5 12.2 reduce-scatter.7
  162.2 14.1 reduce-scatter.3
where the time goes:
time: 209 us; the launch traced here: 208 us
  waiting for transfers between devices  84.5 us (40%)
  matrix products  30 us (14%)
  other arithmetic  28.5 us (14%)
  local copies, waits for them, and re-layouts  17.6 us (8%)
  starting transfers between devices  17 us (8%)
  between operations  15.8 us (8%)
  blocking collectives  14.3 us (7%)
    all_gather x1, waiting for transfers between devices, body(): everything = lax.all_gather(contrib, 'leaf', axis=0, tiled=True)  84.4 us
    dot_general x8, matrix products, body(): term = jnp.einsum('lab,clb->lca', kernel, source_rows[3:], precision=high)  17.4 us
    all_gather x3, blocking collectives, couple(): wide_moments = lax.all_gather(sources, 'col', axis=1, tiled=True)  14.3 us
    ppermute x3, starting transfers between devices, extended_2(): before = lax.ppermute(last, axis, up)  13 us
    reduce_sum x1, other arithmetic, body(): jnp.sum((target[:, :, :, None] - source_rows[:3, :, None, :]) ** 2, axis=0)  11 us
    gather x8, local copies, waits for them, and re-layouts, body(): source_rows = jnp.take(extended, jnp.maximum(column, 0), axis=1)  5.88 us
    dot_general x3, matrix products, couple(): partial_value = jnp.einsum('nsca,nsab->ncb', picked, blocks, precision=high)  4.92 us
    slice x16, local copies, waits for them, and re-layouts, body(): source_rows[:3, :, None, :]  4.28 us
  transfers between devices with their start and end apart: 10, of which 2 were waited for; matrix products, arithmetic and copies ran while one was open for 31% of the time, Pallas kernels for 0%

commit v1 on v0

--- a/solution.py
+++ b/solution.py
@@ -58,7 +58,10 @@
     node_moments = jnp.einsum("lab,lca->cb", leaf_transfer, leaf_moments, precision=high)[None]
     contrib = jnp.einsum("nab,nca->ncb", node_transfer, node_moments, precision=high)
     top_count = lax.axis_size("leaf") // 8
-    everything = lax.all_gather(contrib, "leaf", axis=0, tiled=True)
+    size = lax.axis_size("leaf")
+    pieces = jnp.stack([contrib for _ in range(size)])
+    pieces = lax.all_to_all(pieces, "leaf", split_axis=0, concat_axis=0)
+    everything = jnp.concatenate(pieces, axis=0)
     top_moments = everything.reshape(top_count, 8, core_cols, rank_width).sum(axis=1)
     top_node = device // 8
     top_rows = lax.dynamic_slice_in_dim(top_coupling, top_node, 1, 0)

time: 209 us -> 148 us (0.71)
  waiting for transfers between devices: 84.5 us -> 5.81 us
  starting transfers between devices: 17 us -> 37.7 us
    all_gather x1 -> x0, waiting for transfers between devices: 84.4 us -> none  [body(): everything = lax.all_gather(contrib, 'leaf', axis=0, tiled=True)]
    all_to_all x0 -> x1, starting transfers between devices: none -> 20.7 us  [body(): pieces = lax.all_to_all(pieces, 'leaf', split_axis=0, concat_axis=0)]
    ppermute x3, waiting for transfers between devices: 0.01 us -> 4.53 us  [extended_2(): after = lax.ppermute(leading, axis, down)]
  transfers between devices with their start and end apart: 10 -> 10, of which waited for: 2 -> 3; matrix products, arithmetic and copies ran while one was open for 31% -> 44% of each run, Pallas kernels for 0% -> 0%
where the time goes in v1:
time: 148 us; the launch traced here: 147 us
  starting transfers between devices  37.7 us (25%)
  matrix products  29.4 us (20%)
  other arithmetic  28.4 us (19%)
  local copies, waits for them, and re-layouts  18.8 us (13%)
  between operations  13.9 us (9%)
  blocking collectives  13.5 us (9%)
  waiting for transfers between devices  5.81 us (4%)
    all_to_all x1, starting transfers between devices, body(): pieces = lax.all_to_all(pieces, 'leaf', split_axis=0, concat_axis=0)  20.7 us
    dot_general x8, matrix products, body(): term = jnp.einsum('lab,clb->lca', kernel, source_rows[3:], precision=high)  17.4 us
    all_gather x3, blocking collectives, couple(): wide_moments = lax.all_gather(sources, 'col', axis=1, tiled=True)  13.5 us
    ppermute x3, starting transfers between devices, extended_2(): before = lax.ppermute(last, axis, up)  13 us
    reduce_sum x1, other arithmetic, body(): jnp.sum((target[:, :, :, None] - source_rows[:3, :, None, :]) ** 2, axis=0)  11 us
    gather x8, local copies, waits for them, and re-layouts, body(): source_rows = jnp.take(extended, jnp.maximum(column, 0), axis=1)  5.88 us
    dot_general x3, matrix products, couple(): partial_value = jnp.einsum('nsca,nsab->ncb', picked, blocks, precision=high)  4.91 us
    ppermute x3, waiting for transfers between devices, extended_2(): after = lax.ppermute(leading, axis, down)  4.53 us
  transfers between devices with their start and end apart: 10, of which 3 were waited for; matrix products, arithmetic and copies ran while one was open for 44% of the time, Pallas kernels for 0%

profile of v1, /device:TPU:1, one launch (start us, length us, event | category | flops | bytes accessed | tf_op | source)
XLA Modules:
  0.0 147.4 jit_solution(2955768676463069127)
XLA Ops:
  6.5 1.8 %pad_maximum_fusion.1 = f32[19,2048]{1,0:T(8,128)} fusion(f32[16,2048]{1,0:T(8,128)} %param.15, f32[3,2048]{1,0:T(4,128)} %param.14), kind=kLoop, calls=%fused_computation.99 | loop fusion | flops 38912 | bytes 311296 | tf_op jit(solution)/shard_map/concatenate | solution.py:81
  8.3 5.0 %collective-permute-start = (f32[19,2048]{1,0:T(8,128)}, f32[19,2048]{1,0:T(8,128)}, u32[]{:S(2)}, u32[]{:S(2)}) collective-permute-start(f32[19,2048]{1,0:T(8,128)} %pad_maximum_fusion.1), channel_id=1, source_target_pairs={{0,2},{2,4},{4,6},{6,8},{8,10},{10,12},{12,14},{14,16},{16,18},{18... | collective-permute-start | bytes 466952 | tf_op jit(solution)/shard_map/ppermute | solution.py:17
  13.3 1.3 collective-permute-start.1
  14.6 1.9 %fusion.107 = f32[8,16,128]{2,1,0:T(8,128)S(1)} fusion(f32[8,256,128]{2,1,0:T(8,128)} %param.16, f32[2,8,8,256]{3,2,1,0:T(8,128)} %bitcast.92), kind=kOutput, calls=%fused_computation.109 | convolution fusion | flops 50331648 | bytes 1245184 | tf_op jit(solution)/shard_map/lpr,clp->lcr/dot_general | solution.py:57
  16.6 1.4 fusion.159
  18.1 4.0 %collective-permute-start.4 = (f32[1,16,128]{2,1,0:T(8,128)S(1)}, f32[1,16,128]{2,1,0:T(8,128)S(1)}, u32[]{:S(2)}, u32[]{:S(2)}) collective-permute-start(f32[1,16,128]{2,1,0:T(8,128)S(1)} %bitcast.95), channel_id=1, source_target_pairs={{0,2},{2,4},{4,6},{6,8},{8,10},{10,12},{12,14},{14,16},{16,18},{18... | collective-permute-start | bytes 24584 | tf_op jit(solution)/shard_map/ppermute | solution.py:17
  22.1 1.3 collective-permute-start.5
  23.4 4.0 %collective-permute-start.2 = (f32[8,16,128]{2,1,0:T(8,128)S(1)}, f32[8,16,128]{2,1,0:T(8,128)S(1)}, u32[]{:S(2)}, u32[]{:S(2)}) collective-permute-start(f32[8,16,128]{2,1,0:T(8,128)S(1)} %fusion.107), channel_id=1, source_target_pairs={{0,2},{2,4},{4,6},{6,8},{8,10},{10,12},{12,14},{14,16},{16,18},{18... | collective-permute-start | bytes 196616 | tf_op jit(solution)/shard_map/ppermute | solution.py:17
  27.5 1.1 stack.2
  28.7 20.7 %all-to-all-start = ((f32[128,1,16,128]{3,2,1,0:T(8,128)}), f32[128,1,16,128]{3,2,1,0:T(8,128)}, u32[]{:S(2)}, u32[]{:S(2)}) async-start(f32[128,1,16,128]{3,2,1,0:T(8,128)} %stack.2), calls=%async_computation.2 | async-start | bytes 2097152 | tf_op jit(solution)/shard_map/all_to_all | solution.py:63
  49.7 0.8 convert_reduce_fusion
  59.1 0.7 convert_reduce_fusion.8
  59.8 0.7 compare_reduce_fusion
  60.5 1.3 collective-permute-start.3
  61.8 3.6 %all_gather.10 = f32[3,32,128]{2,1,0:T(8,128)S(1)} all-gather(f32[3,16,128]{2,1,0:T(8,128)S(1)} %pad_maximum_fusion.3), channel_id=1, replica_groups=mesh['leaf'=128,'col'=2] {'col'}, dimensions={1}, use_global_device_ids=true | all-gather | bytes 73728 | tf_op jit(solution)/shard_map/all_gather | solution.py:27
  66.0 0.9 convolution_bitcast_fusion.3
  67.0 4.5 %collective-permute-done.3 = f32[8,16,128]{2,1,0:T(8,128)S(1)} collective-permute-done((f32[8,16,128]{2,1,0:T(8,128)S(1)}, f32[8,16,128]{2,1,0:T(8,128)S(1)}, u32[]{:S(2)}, u32[]{:S(2)}) %collective-permute-start.3) | collective-permute-done | bytes 65568 | tf_op jit(solution)/shard_map/ppermute | solution.py:18
  71.6 4.4 %all_gather.9 = f32[24,32,128]{2,1,0:T(8,128)S(1)} all-gather(f32[24,16,128]{2,1,0:T(8,128)S(1)} %pad_maximum_fusion.2), channel_id=1, replica_groups=mesh['leaf'=128,'col'=2] {'col'}, dimensions={1}, use_global_device_ids=true | all-gather | bytes 589824 | tf_op jit(solution)/shard_map/all_gather | solution.py:27
  76.8 1.2 all-to-all-done
  78.0 1.3 bitcast_reduce_fusion
  79.3 5.5 %all_gather.11 = f32[16,32,128]{2,1,0:T(8,128)S(1)} all-gather(f32[16,16,128]{2,1,0:T(8,128)S(1)} %bitcast_reduce_fusion), channel_id=1, replica_groups=mesh['leaf'=128,'col'=2] {'col'}, dimensions={1}, use_global_device_ids=true | all-gather | bytes 393216 | tf_op jit(solution)/shard_map/all_gather | solution.py:27
  84.9 1.3 gather_fusion.2
  86.2 1.9 %convolution_bitcast_fusion.2 = f32[1,32,128]{2,1,0:T(8,128)} fusion(f32[16,4,64,128]{3,2,1,0:T(8,128)} %param.21, s32[]{:T(128)S(6)} %select_n.66, f32[4,32,64]{2,1,0:T(8,128)} %gather_fusion.2, f32[4]{0:T(128)} %convert_reduce_fusion.8, pred[4]{0:T(512)(128)(4,1)} %compare_reduce_fusion), kind=kOutput, calls=%fused_computation.71 | convolution fusion | flops 12599296 | bytes 214020 | tf_op jit(solution)/shard_map/nsca,nsab->ncb/dot_general | solution.py:32
  88.2 2.1 %convolution_bitcast_fusion = f32[8,32,128]{2,1,0:T(8,128)} fusion(f32[8,8,64,128]{3,2,1,0:T(8,128)S(1)} %copy-done, f32[8,8,32,64]{3,2,1,0:T(8,128)S(1)} %bitcast.89, f32[8,8]{1,0:T(8,128)S(1)} %get-tuple-element.34, pred[8,8]{1,0:T(8,128)(4,1)S(1)} %copy-done.17), kind=kOutput, calls=%fused_computation.68 | convolution fusion | flops 201588736 | bytes 2752832 | tf_op jit(solution)/shard_map/nsca,nsab->ncb/dot_general | solution.py:32
  90.4 1.1 pad_maximum_fusion
  91.9 0.7 gather_fusion.4
  93.3 0.7 gather_fusion.5
  94.7 0.7 gather_fusion.6
  95.5 0.7 copy-done.3
  96.8 0.7 gather_fusion.7
  97.5 0.7 select_bitcast_fusion.3
  98.8 0.7 gather_fusion.8
  100.9 0.7 gather_fusion.9
  103.5 0.8 select_bitcast_fusion.7
  105.6 1.2 gather_fusion.10
  106.8 1.0 select_bitcast_fusion
  107.9 11.0 %multiply_reduce_fusion = (f32[8,256,256]{2,1,0:T(8,128)}, f32[8,256,256]{2,1,0:T(8,128)S(1)}, f32[8,256,256]{2,1,0:T(8,128)S(1)}, f32[8,256,256]{2,1,0:T(8,128)...) fusion(f32[3,8,256]{2,1,0:T(8,128)S(1)} %copy.83, ...), kind=kLoop, calls=%fused_computation.11 | loop fusion | flops 33554432 | bytes 16998400 | tf_op jit(solution)/shard_map/reduce_sum | solution.py:92
  118.9 1.9 %fusion.44 = f32[8,16,256]{2,1,0:T(8,128)S(1)} fusion(f32[8,256,256]{2,1,0:T(8,128)S(1)} %get-tuple-element.7, f32[19,8,256]{2,0,1:T(8,128)S(1)} %select_bitcast_fusion.6, f32[8]{0:T(128)S(1)} %copy-done.26), kind=kOutput, calls=%fused_computation.55 | convolution fusion | flops 101744640 | bytes 2359808 | tf_op jit(solution)/shard_map/lab,clb->lca/dot_general | solution.py:94
  120.8 1.9 %fusion.47 = f32[8,16,256]{2,1,0:T(8,128)S(1)} fusion(f32[8,256,256]{2,1,0:T(8,128)S(1)} %get-tuple-element.8, f32[19,8,256]{2,0,1:T(8,128)S(1)} %select_bitcast_fusion.5, f32[8]{0:T(128)S(1)} %copy-done.25), kind=kOutput, calls=%fused_computation.56 | convolution fusion | flops 101744640 | bytes 2359808 | tf_op jit(solution)/shard_map/lab,clb->lca/dot_general | solution.py:94
  122.8 1.9 %fusion.50 = f32[8,16,256]{2,1,0:T(8,128)S(1)} fusion(f32[8,256,256]{2,1,0:T(8,128)S(1)} %get-tuple-element.9, f32[19,8,256]{2,0,1:T(8,128)S(1)} %copy-done.4, f32[8]{0:T(128)S(1)} %copy-done.24), kind=kOutput, calls=%fused_computation.57 | convolution fusion | flops 101744640 | bytes 2359808 | tf_op jit(solution)/shard_map/lab,clb->lca/dot_general | solution.py:94
  124.7 1.9 %fusion.65 = f32[8,16,256]{2,1,0:T(8,128)S(1)} fusion(f32[8,256,256]{2,1,0:T(8,128)S(1)} %get-tuple-element.11, f32[19,8,256]{2,0,1:T(8,128)S(1)} %copy-done.6, f32[8]{0:T(128)S(1)} %copy-done.23), kind=kOutput, calls=%fused_computation.62 | convolution fusion | flops 101744640 | bytes 2359808 | tf_op jit(solution)/shard_map/lab,clb->lca/dot_general | solution.py:94
  126.6 1.9 %fusion.68 = f32[8,16,256]{2,1,0:T(8,128)S(1)} fusion(f32[8,256,256]{2,1,0:T(8,128)S(1)} %get-tuple-element.12, f32[19,8,256]{2,0,1:T(8,128)S(1)} %copy-done.8, f32[8]{0:T(128)S(1)} %copy-done.22), kind=kOutput, calls=%fused_computation.63 | convolution fusion | flops 101744640 | bytes 2359808 | tf_op jit(solution)/shard_map/lab,clb->lca/dot_general | solution.py:94
  128.6 1.9 %fusion.41 = f32[8,16,256]{2,1,0:T(8,128)S(1)} fusion(f32[8,16,256]{2,1,0:T(8,128)S(1)} %fusion.50, f32[8,16,256]{2,1,0:T(8,128)S(1)} %fusion.47, f32[8,16,256]{2,1,0:T(8,128)S(1)} %fusion.44, f32[8,256,256]{2,1,0:T(8,128)S(1)} %get-tuple-element.13, f32[19,8,256]{2,0,1:T(8,128)S(1)} %copy-done.10, f32[8]{0:T(128)S(1)} %copy-done.21), kind=kOutput, calls=%fused_computation.54 | convolution fusion | flops 101842944 | bytes 2753024 | tf_op jit(solution)/shard_map/lab,clb->lca/dot_general | solution.py:94
  130.5 2.6 %fusion.62 = f32[8,16,256]{2,1,0:T(8,128)} fusion(f32[8,16,256]{2,1,0:T(8,128)S(1)} %fusion.68, f32[8,16,256]{2,1,0:T(8,128)S(1)} %fusion.65, f32[8,16,256]{2,1,0:T(8,128)S(1)} %fusion.41, f32[8,256,256]{2,1,0:T(8,128)S(1)} %get-tuple-element.10, f32[19,8,256]{2,0,1:T(8,128)S(1)} %select_bitcast_fusion.3, f32[8]{0:T(128)S(1)} %copy-done.20), kind=kOutput, calls=%fused_computation.61 | convolution fusion | flops 101842944 | bytes 2753024 | tf_op jit(solution)/shard_map/lab,clb->lca/dot_general | solution.py:94
  133.1 1.0 fusion.85
  134.1 1.6 %fusion.83 = f32[8,16,128]{2,1,0:T(8,128)S(1)} fusion(f32[8,16,128]{2,1,0:T(8,128)} %reduce-scatter.4.cloned.1.call-done, f32[16,128,1]{1,0,2:T(8,128)S(1)} %fusion.85, f32[8,128,128]{2,1,0:T(8,128)} %param.17), kind=kOutput, calls=%fused_computation.70 | convolution fusion | flops 25182208 | bytes 663552 | tf_op jit(solution)/shard_map/lab,cb->lca/dot_general | solution.py:77
  135.7 1.0 fusion.160
  136.7 3.5 %fusion.80 = f32[8,2,8,256]{3,2,1,0:T(8,128)S(1)} fusion(f32[8,16,256]{2,1,0:T(8,128)S(1)} %fusion.160, f32[8,16,256]{2,1,0:T(8,128)} %fusion.62, f32[8,256,256]{2,1,0:T(8,128)} %get-tuple-element.6, f32[19,8,256]{2,0,1:T(8,128)S(1)} %select_bitcast_fusion, f32[8]{0:T(128)S(1)} %copy-done.32), kind=kOutput, calls=%fused_computation.67 | convolution fusion | flops 101810176 | bytes 2621952 | tf_op jit(solution)/shard_map/lab,clb->lca/dot_general | solution.py:94
  (144 shorter events, 19.3 us)
Async XLA Ops:
  6.5 81.6 %copy-start = (f32[8,8,64,128]{3,2,1,0:T(8,128)S(1)}, f32[8,8,64,128]{3,2,1,0:T(8,128)}, u32[]{:S(2)}) copy-start(f32[8,8,64,128]{3,2,1,0:T(8,128)} %param.19) | copy-start | bytes 6291460
  6.5 20.8 %copy-start.13 = (f32[1,128,128]{2,1,0:T(8,128)S(1)}, f32[1,128,128]{2,1,0:T(8,128)}, u32[]{:S(2)}) copy-start(f32[1,128,128]{2,1,0:T(8,128)} %param.18) | copy-start | bytes 196612
  8.3 82.0 %collective-permute-start = (f32[19,2048]{1,0:T(8,128)}, f32[19,2048]{1,0:T(8,128)}, u32[]{:S(2)}, u32[]{:S(2)}) collective-permute-start(f32[19,2048]{1,0:T(8,128)} %pad_maximum_fusion.1), channel_id=1, source_target_pairs={{0,2},{2,4},{4,6},{6,8},{8,10},{10,12},{12,14},{14,16},{16,18},{18... | collective-permute-start | bytes 466952 | tf_op jit(solution)/shard_map/ppermute | solution.py:17
  13.3 77.0 %collective-permute-start.1 = (f32[19,2048]{1,0:T(8,128)}, f32[19,2048]{1,0:T(8,128)}, u32[]{:S(2)}, u32[]{:S(2)}) collective-permute-start(f32[19,2048]{1,0:T(8,128)} %pad_maximum_fusion.1), channel_id=1, source_target_pairs={{2,0},{4,2},{6,4},{8,6},{10,8},{12,10},{14,12},{16,14},{18,16},{20... | collective-permute-start | bytes 466952 | tf_op jit(solution)/shard_map/ppermute | solution.py:18
  16.6 32.9 %copy-start.19 = (s32[8,8]{1,0:T(8,128)S(1)}, s32[8,8]{1,0:T(8,128)}, u32[]{:S(2)}) copy-start(s32[8,8]{1,0:T(8,128)} %param.22) | copy-start | bytes 772
  16.6 38.2 %copy-start.16 = (s32[16,4]{0,1:T(4,128)S(1)}, s32[16,4]{0,1:T(4,128)}, u32[]{:S(2)}) copy-start(s32[16,4]{0,1:T(4,128)} %param.25) | copy-start | bytes 772
  16.6 39.0 %copy-start.33 = (s32[1,2]{1,0:T(1,128)S(1)}, s32[1,2]{1,0:T(1,128)}, u32[]{:S(2)}) copy-start(s32[1,2]{1,0:T(1,128)} %param.24) | copy-start | bytes 28
  16.6 39.0 %copy-start.18 = (s32[8,8]{1,0:T(8,128)S(1)}, s32[8,8]{1,0:T(8,128)}, u32[]{:S(2)}) copy-start(s32[8,8]{1,0:T(8,128)} %param.23) | copy-start | bytes 772
  16.6 41.9 %copy-start.11 = (f32[3,2048]{1,0:T(4,128)S(1)}, f32[3,2048]{1,0:T(4,128)}, u32[]{:S(2)}) copy-start(f32[3,2048]{1,0:T(4,128)} %param.14) | copy-start | bytes 73732
  16.6 49.4 %copy-start.15 = (f32[1,2,64,128]{3,2,1,0:T(8,128)S(1)}, f32[1,2,64,128]{3,2,1,0:T(8,128)}, u32[]{:S(2)}) copy-start(f32[1,2,64,128]{3,2,1,0:T(8,128)} %param.20) | copy-start | bytes 196612
  18.1 42.4 %collective-permute-start.4 = (f32[1,16,128]{2,1,0:T(8,128)S(1)}, f32[1,16,128]{2,1,0:T(8,128)S(1)}, u32[]{:S(2)}, u32[]{:S(2)}) collective-permute-start(f32[1,16,128]{2,1,0:T(8,128)S(1)} %bitcast.95), channel_id=1, source_target_pairs={{0,2},{2,4},{4,6},{6,8},{8,10},{10,12},{12,14},{14,16},{16,18},{18... | collective-permute-start | bytes 24584 | tf_op jit(solution)/shard_map/ppermute | solution.py:17
  22.1 39.7 %collective-permute-start.5 = (f32[1,16,128]{2,1,0:T(8,128)S(1)}, f32[1,16,128]{2,1,0:T(8,128)S(1)}, u32[]{:S(2)}, u32[]{:S(2)}) collective-permute-start(f32[1,16,128]{2,1,0:T(8,128)S(1)} %bitcast.96), channel_id=1, source_target_pairs={{2,0},{4,2},{6,4},{8,6},{10,8},{12,10},{14,12},{16,14},{18,16},{20... | collective-permute-start | bytes 24584 | tf_op jit(solution)/shard_map/ppermute | solution.py:18
  23.4 43.6 %collective-permute-start.2 = (f32[8,16,128]{2,1,0:T(8,128)S(1)}, f32[8,16,128]{2,1,0:T(8,128)S(1)}, u32[]{:S(2)}, u32[]{:S(2)}) collective-permute-start(f32[8,16,128]{2,1,0:T(8,128)S(1)} %fusion.107), channel_id=1, source_target_pairs={{0,2},{2,4},{4,6},{6,8},{8,10},{10,12},{12,14},{14,16},{16,18},{18... | collective-permute-start | bytes 196616 | tf_op jit(solution)/shard_map/ppermute | solution.py:17
  28.7 49.3 %all-to-all-start = ((f32[128,1,16,128]{3,2,1,0:T(8,128)}), f32[128,1,16,128]{3,2,1,0:T(8,128)}, u32[]{:S(2)}, u32[]{:S(2)}) async-start(f32[128,1,16,128]{3,2,1,0:T(8,128)} %stack.2), calls=%async_computation.2 | async-start | bytes 2097152 | tf_op jit(solution)/shard_map/all_to_all | solution.py:63
  49.4 83.7 %reduce-scatter.6.cloned.1.call-start = ((), (), s32[]{:S(2)}) async-start(), calls=%async_computation.5 | async-start | bytes 24576 | tf_op jit(solution)/shard_map/reduce_scatter | solution.py:33
  60.5 11.0 %collective-permute-start.3 = (f32[8,16,128]{2,1,0:T(8,128)S(1)}, f32[8,16,128]{2,1,0:T(8,128)S(1)}, u32[]{:S(2)}, u32[]{:S(2)}) collective-permute-start(f32[8,16,128]{2,1,0:T(8,128)S(1)} %fusion.107), channel_id=1, source_target_pairs={{2,0},{4,2},{6,4},{8,6},{10,8},{12,10},{14,12},{16,14},{18,16},{20... | collective-permute-start | bytes 196616 | tf_op jit(solution)/shard_map/ppermute | solution.py:18
  67.0 66.1 %reduce-scatter.8.cloned.1.call-start = ((), (), s32[]{:S(2)}) async-start(), calls=%async_computation.6 | async-start | bytes 24576 | tf_op jit(solution)/shard_map/reduce_scatter | solution.py:33
  76.8 11.4 %copy-start.17 = (pred[8,8]{1,0:T(8,128)(4,1)S(1)}, pred[8,8]{1,0:T(8,128)(4,1)}, u32[]{:S(2)}) copy-start(pred[8,8]{1,0:T(8,128)(4,1)} %get-tuple-element.32) | copy-start | bytes 196
  84.8 5.6 %copy-start.2 = (f32[16,2048]{1,0:T(8,128)S(1)}, f32[16,2048]{1,0:T(8,128)}, u32[]{:S(2)}) copy-start(f32[16,2048]{1,0:T(8,128)} %param.15) | copy-start | bytes 393220
  86.2 4.2 %copy-start.12 = (f32[3,2048]{1,0:T(4,128)S(1)}, f32[3,2048]{1,0:T(4,128)}, u32[]{:S(2)}) copy-start(f32[3,2048]{1,0:T(4,128)} %param.14) | copy-start | bytes 73732
  88.1 46.0 %reduce-scatter.4.cloned.1.call-start = ((), (), s32[]{:S(2)}) async-start(), calls=%async_computation.4 | async-start | bytes 196608 | tf_op jit(solution)/shard_map/reduce_scatter | solution.py:33
  90.3 2.3 %copy-start.31 = (pred[8]{0:T(512)(128)(4,1)S(1)}, pred[8]{0:T(512)(128)(4,1)}, u32[]{:S(2)}) copy-start(pred[8]{0:T(512)(128)(4,1)} %get-tuple-element.48) | copy-start | bytes 28
  91.5 2.6 %copy-start.30 = (pred[8]{0:T(512)(128)(4,1)S(1)}, pred[8]{0:T(512)(128)(4,1)}, u32[]{:S(2)}) copy-start(pred[8]{0:T(512)(128)(4,1)} %get-tuple-element.47) | copy-start | bytes 28
  91.7 3.8 %copy-start.29 = (pred[8]{0:T(512)(128)(4,1)S(1)}, pred[8]{0:T(512)(128)(4,1)}, u32[]{:S(2)}) copy-start(pred[8]{0:T(512)(128)(4,1)} %get-tuple-element.46) | copy-start | bytes 28
  91.7 7.8 %copy-start.28 = (pred[8]{0:T(512)(128)(4,1)S(1)}, pred[8]{0:T(512)(128)(4,1)}, u32[]{:S(2)}) copy-start(pred[8]{0:T(512)(128)(4,1)} %get-tuple-element.44) | copy-start | bytes 28
  92.6 9.0 %copy-start.27 = (pred[8]{0:T(512)(128)(4,1)S(1)}, pred[8]{0:T(512)(128)(4,1)}, u32[]{:S(2)}) copy-start(pred[8]{0:T(512)(128)(4,1)} %get-tuple-element.43) | copy-start | bytes 28
  95.5 0.7 copy-start.3
  96.2 11.7 %copy-start.14 = (f32[1,3,8,256]{3,2,1,0:T(8,128)S(1)}, f32[1,3,8,256]{3,2,1,0:T(8,128)}, u32[]{:S(2)}) copy-start(f32[1,3,8,256]{3,2,1,0:T(8,128)} %copy.96) | copy-start | bytes 73732
  99.6 0.7 copy-start.5
  101.7 0.7 copy-start.7
  104.3 0.7 copy-start.9
  107.9 11.0 %copy-start.26 = (f32[8]{0:T(128)S(1)}, f32[8]{0:T(128)}, u32[]{:S(2)}) copy-start(f32[8]{0:T(128)} %get-tuple-element.20) | copy-start | bytes 100
  118.9 1.9 %copy-start.25 = (f32[8]{0:T(128)S(1)}, f32[8]{0:T(128)}, u32[]{:S(2)}) copy-start(f32[8]{0:T(128)} %get-tuple-element.19) | copy-start | bytes 100
  118.9 3.8 %copy-start.4 = (f32[19,8,256]{2,0,1:T(8,128)S(1)}, f32[19,8,256]{2,0,1:T(8,128)}, u32[]{:S(2)}) copy-start(f32[19,8,256]{2,0,1:T(8,128)} %copy-done.3) | copy-start | bytes 466948
  118.9 3.8 %copy-start.24 = (f32[8]{0:T(128)S(1)}, f32[8]{0:T(128)}, u32[]{:S(2)}) copy-start(f32[8]{0:T(128)} %get-tuple-element.18) | copy-start | bytes 100
  120.8 3.9 %copy-start.6 = (f32[19,8,256]{2,0,1:T(8,128)S(1)}, f32[19,8,256]{2,0,1:T(8,128)}, u32[]{:S(2)}) copy-start(f32[19,8,256]{2,0,1:T(8,128)} %copy-done.5) | copy-start | bytes 466948
  120.8 3.9 %copy-start.23 = (f32[8]{0:T(128)S(1)}, f32[8]{0:T(128)}, u32[]{:S(2)}) copy-start(f32[8]{0:T(128)} %get-tuple-element.16) | copy-start | bytes 100
  122.8 3.9 %copy-start.8 = (f32[19,8,256]{2,0,1:T(8,128)S(1)}, f32[19,8,256]{2,0,1:T(8,128)}, u32[]{:S(2)}) copy-start(f32[19,8,256]{2,0,1:T(8,128)} %copy-done.7) | copy-start | bytes 466948
  122.8 3.9 %copy-start.22 = (f32[8]{0:T(128)S(1)}, f32[8]{0:T(128)}, u32[]{:S(2)}) copy-start(f32[8]{0:T(128)} %get-tuple-element.15) | copy-start | bytes 100
  124.7 3.8 %copy-start.10 = (f32[19,8,256]{2,0,1:T(8,128)S(1)}, f32[19,8,256]{2,0,1:T(8,128)}, u32[]{:S(2)}) copy-start(f32[19,8,256]{2,0,1:T(8,128)} %copy-done.9) | copy-start | bytes 466948
  124.7 3.8 %copy-start.21 = (f32[8]{0:T(128)S(1)}, f32[8]{0:T(128)}, u32[]{:S(2)}) copy-start(f32[8]{0:T(128)} %get-tuple-element.21) | copy-start | bytes 100
  126.6 3.9 %copy-start.20 = (f32[8]{0:T(128)S(1)}, f32[8]{0:T(128)}, u32[]{:S(2)}) copy-start(f32[8]{0:T(128)} %get-tuple-element.17) | copy-start | bytes 100
  130.5 5.3 %copy-start.1 = (f32[8,256,128]{2,1,0:T(8,128)S(1)}, f32[8,256,128]{2,1,0:T(8,128)}, u32[]{:S(2)}) copy-start(f32[8,256,128]{2,1,0:T(8,128)} %param.16) | copy-start | bytes 3145732
  130.5 6.2 %copy-start.32 = (f32[8]{0:T(128)S(1)}, f32[8]{0:T(128)}, u32[]{:S(2)}) copy-start(f32[8]{0:T(128)} %get-tuple-element.14) | copy-start | bytes 100
Sparse Core Ops, SparseCore 0:
  67.1 15.3 reduce-scatter.5
  88.2 10.7 reduce-scatter.7
  101.5 14.1 reduce-scatter.3
